TPU v7x, 512 devices: a whole 4x4x16 slice. The times are simulated.
512 devices in a mesh: row: 32 (over x, z_lo, core), col: 16 (over y, z_hi).
Axes of the slice: x: 4, y: 4, z: 16 (z_hi: 4, z_lo: 4; z = z_hi * 4 + z_lo), core: 2. Of those that a mesh axis runs over, the one named last changes fastest.
Arguments:
- hidden_img: bfloat16 [16384, 2432], P('row', 'col'), may hold values from -75 to 75
- hidden_txt: bfloat16 [3072, 2432], P('row', 'col'), may hold values from -75 to 75
- text_len: int32 [16], replicated, may hold values from 1 to 154, as said below
- step_index: int32 [16], replicated, may hold values from 0 to 27
- latent: float32 [16384, 64], P('row'), may hold values from -6 to 6
- cond: float32 [16, 2432], P(None, 'row'), may hold values from -6 to 6
- mod_weight: bfloat16 [2432, 7, 2432], P('row', None, 'col'), may hold values from -0.125 to 0.125
- qkv_weight: bfloat16 [2432, 3, 2048], P('row', None, 'col'), may hold values from -0.125 to 0.125
- kv_text_weight: bfloat16 [2432, 2, 2048], P('row', None, 'col'), may hold values from -0.125 to 0.125
- q_gain: float32 [64], replicated, may hold values from 0.5 to 6
- k_gain: float32 [2, 64], replicated, may hold values from 0.5 to 6
- out_weight: bfloat16 [2048, 2432], P('row', 'col'), may hold values from -6 to 6
- final_weight: bfloat16 [2432, 64], P('row'), may hold values from -0.125 to 0.125
Outputs:
- velocity: float32 [16384, 64], P('row')
- latent_next: float32 [16384, 64], P('row')
Inputs may be any that keep to these rules, and one draw needn't show every extreme that they name: `text_len`: some request has exactly 154 text tokens in every draw.
All inputs are finite; a program needn't handle non-finite values.
Results may differ from a plain program's by a relative error of at most 0.015.
The roundings to bfloat16 on the way count: a program that leaves them out, or rounds other values in their place, can miss the bound.
Values may be sent and summed in bfloat16 or wider, within the bound.
A program may use at most 64 MiB of HBM per device.

v0:
```python
import jax
import jax.numpy as jnp
from jax import lax
from jax.sharding import PartitionSpec as P

STEPS = 28
EPS_NORM = 1e-06


def partner_2(block, axis, distance):
    count = lax.axis_size(axis)
    route = []
    for low in range(count):
        high = low | 1 << distance
        if high != low and high < count:
            route += [(low, high), (high, low)]
    return lax.ppermute(block, axis, route)


def modulate_full(values, offset, stretch):
    average = jnp.mean(values, axis=1, keepdims=True)
    mean_square = jnp.mean(values * values, axis=1, keepdims=True)
    normed = (values - average) * lax.rsqrt(mean_square - average * average + EPS_NORM)
    return (normed * (1.0 + stretch) + offset).astype(jnp.bfloat16)


def head_norm(values, gain_row):
    mean_square = jnp.mean(values * values, axis=-1, keepdims=True)
    return (values * lax.rsqrt(mean_square + EPS_NORM) * gain_row).astype(jnp.bfloat16)


def sigma_of(step_now):
    remain = 1.0 - step_now.astype(jnp.float32) / STEPS
    return 3.0 * remain / (1.0 + 2.0 * remain)


def per_device(
    hidden_img,
    hidden_txt,
    text_len,
    step_index,
    latent,
    cond,
    mod_weight,
    qkv_weight,
    kv_text_weight,
    q_gain,
    k_gain,
    out_weight,
    final_weight,
):
    row_pos = lax.axis_index("row")
    request = row_pos // 2
    lower_half = row_pos % 2 == 0
    img_rows, width_part = hidden_img.shape
    txt_rows = hidden_txt.shape[0]
    head_dim = q_gain.shape[0]
    qkv_cols = qkv_weight.shape[2]
    heads_here = qkv_cols // head_dim
    activated = jax.nn.silu(cond).astype(jnp.bfloat16)
    mod_local = mod_weight.reshape(mod_weight.shape[0], 7 * width_part)
    mod_terms = jnp.dot(activated, mod_local, preferred_element_type=jnp.float32).reshape(
        activated.shape[0], 7, width_part
    )
    mod_all = lax.psum(mod_terms, "row")
    mod_own = lax.dynamic_index_in_dim(mod_all, request, 0, keepdims=False)
    mod_full = lax.all_gather(mod_own, "col", axis=1, tiled=True)
    img_full, txt_full = (
        lax.all_gather(hidden_img, "col", axis=1, tiled=True),
        lax.all_gather(hidden_txt, "col", axis=1, tiled=True),
    )
    img_ready = modulate_full(img_full.astype(jnp.float32), mod_full[0], mod_full[1])
    txt_ready = modulate_full(txt_full.astype(jnp.float32), mod_full[3], mod_full[4])
    qkv_flat = qkv_weight.reshape(qkv_weight.shape[0], 3 * qkv_cols)
    kv_flat = kv_text_weight.reshape(kv_text_weight.shape[0], 2 * qkv_cols)
    img_proj = jnp.dot(
        img_ready,
        lax.all_gather(qkv_flat, "row", axis=0, tiled=True),
        preferred_element_type=jnp.float32,
    )
    txt_proj = jnp.dot(
        txt_ready,
        lax.all_gather(kv_flat, "row", axis=0, tiled=True),
        preferred_element_type=jnp.float32,
    )
    img_proj = img_proj.reshape(img_rows, 3, heads_here, head_dim)
    txt_proj = txt_proj.reshape(txt_rows, 2, heads_here, head_dim)
    queries = head_norm(img_proj[:, 0], q_gain)
    img_keys = head_norm(img_proj[:, 1], k_gain[0])
    img_values = img_proj[:, 2].astype(jnp.bfloat16)
    txt_keys = head_norm(txt_proj[:, 0], k_gain[1])
    txt_values = txt_proj[:, 1].astype(jnp.bfloat16)
    length = lax.dynamic_index_in_dim(text_len, request, 0, keepdims=False)
    scaling = head_dim ** (-0.5)
    partner = partner_2((img_keys, img_values, txt_keys, txt_values), "row", 0)

    def ordered(own_part, peer_part):
        return jnp.concatenate(
            [
                jnp.where(lower_half, own_part, peer_part),
                jnp.where(lower_half, peer_part, own_part),
            ],
            axis=0,
        )

    all_keys = jnp.concatenate(
        [ordered(img_keys, partner[0]), ordered(txt_keys, partner[2])], axis=0
    )
    all_values = jnp.concatenate(
        [ordered(img_values, partner[1]), ordered(txt_values, partner[3])], axis=0
    )
    key_valid = jnp.concatenate(
        [jnp.ones((2 * img_rows,), dtype=bool), jnp.arange(2 * txt_rows) < length]
    )

    def attend(head_ops):
        q_head, k_head, v_head = head_ops
        scores = jnp.dot(q_head, k_head.T, preferred_element_type=jnp.float32) * scaling
        scores = jnp.where(key_valid[None, :], scores, -jnp.inf)
        row_max = jnp.max(scores, axis=1, keepdims=True)
        weights = jnp.exp(scores - row_max)
        probabilities = (weights / jnp.sum(weights, axis=1, keepdims=True)).astype(jnp.bfloat16)
        return jnp.dot(probabilities, v_head, preferred_element_type=jnp.float32).astype(
            jnp.bfloat16
        )

    attended = lax.map(
        attend,
        (jnp.moveaxis(queries, 1, 0), jnp.moveaxis(all_keys, 1, 0), jnp.moveaxis(all_values, 1, 0)),
    )
    attended = jnp.moveaxis(attended, 0, 1).reshape(img_rows, qkv_cols)
    full_heads = lax.all_gather(attended, "col", axis=1, tiled=True)
    projected = jnp.dot(
        full_heads,
        lax.all_gather(out_weight, "row", axis=0, tiled=True),
        preferred_element_type=jnp.float32,
    )
    updated = (hidden_img.astype(jnp.float32) + mod_own[2] * projected).astype(jnp.bfloat16)
    head_full = lax.all_gather(final_weight, "row", axis=0, tiled=True)
    residual = lax.all_gather(updated, "col", axis=1, tiled=True)
    head_in = modulate_full(residual.astype(jnp.float32), mod_full[5], mod_full[6])
    velocity = jnp.dot(head_in, head_full, preferred_element_type=jnp.float32)
    step_now = lax.dynamic_index_in_dim(step_index, request, 0, keepdims=False)
    sigma_step = sigma_of(step_now + 1) - sigma_of(step_now)
    latent_next = latent + sigma_step * velocity
    return (velocity, latent_next)


def solution(mesh):
    in_specs = (
        P("row", "col"),
        P("row", "col"),
        P(),
        P(),
        P("row", None),
        P(None, "row"),
        P("row", None, "col"),
        P("row", None, "col"),
        P("row", None, "col"),
        P(),
        P(),
        P("row", "col"),
        P("row", None),
    )
    out_specs = (P("row", None), P("row", None))
    return jax.shard_map(
        per_device, mesh=mesh, in_specs=in_specs, out_specs=out_specs, check_vma=False
    )
```

profile of v0, /device:TPU:1, one launch (start us, length us, event | category | flops | bytes accessed | tf_op | source)
XLA Modules:
  0.0 753.6 jit_solution(9680876865259763626)
XLA Ops:
  7.2 0.0 all-reduce.3.cloned.1.call-start
  7.2 0.9 copy-done
  8.1 1.6 fusion.48
  9.7 0.0 all-reduce.3.cloned.1.call-update
  9.8 0.0 all-gather.18.cloned.1.call-start
  9.8 1.4 reshape.166
  11.2 0.0 all-gather.18.cloned.1.call-update
  11.3 0.0 all-gather.16.cloned.1.call-start
  11.3 0.9 copy.53
  12.2 0.7 reshape.164
  12.9 0.0 all-gather.16.cloned.1.call-update
  12.9 0.0 all-gather.10.cloned.1.call-start
  12.9 0.5 all-gather.10.cloned.1.call-update
  13.5 0.0 all-gather.12.cloned.1.call-start
  13.6 1.2 dynamic_slice.23
  14.8 0.6 iota_compare_fusion
  15.4 61.1 %all_gather.30 = bf16[96,2432]{0,1:T(8,128)(2,1)S(1)} all-gather(bf16[96,152]{0,1:T(8,128)(2,1)} %param.16), channel_id=1, replica_groups=mesh['row'=32,'col'=16] {'col'}, dimensions={1}, use_global_device_ids=true | all-gather | bytes 496128 | tf_op jit(solution)/shard_map/all_gather | solution.py:70
  76.5 0.3 convert_reduce_fusion.2
  76.8 1.3 slice_bitcast_fusion.3
  78.1 199.8 %all-reduce.3.cloned.1.call-done = f32[16,7,152]{2,0,1:T(8,128)} async-done(((f32[16,7,152]{2,0,1:T(8,128)}), f32[16,7,152]{2,0,1:T(8,128)}) %all-reduce.3.cloned.1.call-update) | async-done | bytes 68112 | tf_op jit(solution)/shard_map/psum | solution.py:65
  277.9 0.8 constant_dynamic-slice_fusion.1
  278.7 0.1 copy.52
  278.8 77.3 %all-gather = f32[1,7,2432]{1,0,2:T(1,128)S(1)} all-gather(f32[1,7,152]{1,0,2:T(1,128)S(1)} %copy.52), channel_id=2, replica_groups=mesh['row'=32,'col'=16] {'col'}, dimensions={2}, use_global_device_ids=true | all-gather | bytes 72352 | tf_op jit(solution)/shard_map/all_gather | solution.py:67
  356.1 42.9 %fusion.39 = (f32[2432]{0:T(1024)}, f32[2432]{0:T(1024)S(1)}, f32[2432]{0:T(1024)S(1)}, f32[2432]{0:T(1024)}, f32[2432]{0:T(1024)}, /*index=5*/f32[2432]{0:T(1024)}) fusion(f32[1,7,2432]{1,0,2:T(1,128)S(1)} %all-gather), kind=kLoop, calls=%fused_computation.55 | loop fusion | flops 7296 | bytes 116736 | tf_op jit(solution)/shard_map/add | solution.py:24
  399.0 2.2 reshape.167
  401.1 1.3 fusion.42
  402.4 6.7 collective-permute-start.3
  409.2 0.1 multiply_convert_fusion.2
  409.2 1.9 collective-permute-start.1
  411.2 0.6 broadcast_select_fusion.4
  411.8 0.5 collective-permute-done.1
  412.3 0.7 broadcast_select_fusion.6
  413.1 14.4 %all-gather.16.cloned.1.call-done = bf16[32,76,384]{2,1,0:T(8,128)(2,1)} async-done(((bf16[1,76,384]{2,1,0:T(8,128)(2,1)}), bf16[32,76,384]{2,1,0:T(8,128)(2,1)}) %all-gather.16.cloned.1.call-update) | async-done | bytes 1867792 | tf_op jit(solution)/shard_map/all_gather | solution.py:78
  427.5 2.5 reshape.165
  429.9 103.8 %all-gather.10.cloned.1.call-done = bf16[512,2432]{0,1:T(8,128)(2,1)} async-done(((bf16[512,152]{0,1:T(8,128)(2,1)}), bf16[512,2432]{0,1:T(8,128)(2,1)}) %all-gather.10.cloned.1.call-update) | async-done | bytes 2490384 | tf_op jit(solution)/shard_map/all_gather | solution.py:69
  533.7 2.6 convert_reduce_fusion.1
  536.4 1.9 fusion.24
  538.3 0.1 multiply_reduce_fusion
  538.4 0.1 multiply_convert_fusion
  538.5 2.8 collective-permute-start
  541.3 2.1 collective-permute-start.2
  543.5 0.9 concatenate.10
  544.4 0.4 collective-permute-done.2
  544.8 0.1 concatenate.11
  544.9 3.1 while.10
  544.9 0.5 fusion.66
  545.5 0.4 fusion.67
  545.9 0.6 fusion.68
  546.5 0.6 fusion.66
  547.0 0.4 fusion.67
  547.4 0.6 fusion.68
  548.0 0.6 copy-done.4
  548.7 0.0 all-gather.14.cloned.1.call-start
  548.7 44.3 %all_gather.33 = bf16[2048,152]{1,0:T(8,128)(2,1)S(1)} all-gather(bf16[64,152]{1,0:T(8,128)(2,1)S(1)} %copy-done.6), channel_id=1, replica_groups=mesh['row'=32,'col'=16] {'row'}, dimensions={0}, use_global_device_ids=true | all-gather | bytes 642048 | tf_op jit(solution)/shard_map/all_gather | solution.py:135
  593.1 0.7 constant_dynamic-slice_fusion
  593.8 45.6 %all-gather.12.cloned.1.call-done = bf16[512,2048]{0,1:T(8,128)(2,1)} async-done(((bf16[512,128]{0,1:T(8,128)(2,1)}), bf16[512,2048]{0,1:T(8,128)(2,1)}) %all-gather.12.cloned.1.call-update) | async-done | bytes 2097168 | tf_op jit(solution)/shard_map/all_gather | solution.py:132
  639.4 2.8 fusion.41
  642.3 0.6 dynamic_slice.24
  644.2 45.2 %all-gather.3 = bf16[32,76,64]{1,2,0:T(8,128)(2,1)S(1)} all-gather(bf16[1,76,64]{1,2,0:T(8,128)(2,1)S(1)} %bitcast.104), channel_id=1, replica_groups=mesh['row'=32,'col'=16] {'row'}, dimensions={0}, use_global_device_ids=true | all-gather | bytes 321024 | tf_op jit(solution)/shard_map/all_gather | solution.py:139
  689.4 0.3 copy.58
  689.8 0.8 reshape.169
  690.6 51.6 %all-gather.14.cloned.1.call-done = bf16[512,2432]{0,1:T(8,128)(2,1)} async-done(((bf16[512,152]{0,1:T(8,128)(2,1)}), bf16[512,2432]{0,1:T(8,128)(2,1)}) %all-gather.14.cloned.1.call-update) | async-done | bytes 2490384 | tf_op jit(solution)/shard_map/all_gather | solution.py:140
  742.3 2.6 convert_reduce_fusion
  744.9 1.8 multiply_add_fusion
  (47 shorter events, 0.3 us)
Async XLA Ops:
  7.2 1.0 copy-start
  7.2 270.7 %all-reduce.3.cloned.1.call-start = ((), (), s32[]{:S(2)}) async-start(), calls=%async_computation | async-start | bytes 229376 | tf_op jit(solution)/shard_map/psum | solution.py:65
  9.8 389.2 %all-gather.18.cloned.1.call-start = ((), (), s32[]{:S(2)}) async-start(), calls=%async_computation.5 | async-start | bytes 1351680 | tf_op jit(solution)/shard_map/all_gather | solution.py:83
  11.3 416.2 %all-gather.16.cloned.1.call-start = ((), (), s32[]{:S(2)}) async-start(), calls=%async_computation.4 | async-start | bytes 2027520 | tf_op jit(solution)/shard_map/all_gather | solution.py:78
  12.9 520.9 %all-gather.10.cloned.1.call-start = ((), (), s32[]{:S(2)}) async-start(), calls=%async_computation.1 | async-start | bytes 2646016 | tf_op jit(solution)/shard_map/all_gather | solution.py:69
  13.5 626.0 %all-gather.12.cloned.1.call-start = ((), (), s32[]{:S(2)}) async-start(), calls=%async_computation.2 | async-start | bytes 2228224 | tf_op jit(solution)/shard_map/all_gather | solution.py:132
  402.4 8.8 %collective-permute-start.3 = (bf16[96,2,64]{0,2,1:T(8,128)(2,1)S(1)}, bf16[96,2,64]{0,2,1:T(8,128)(2,1)S(1)}, u32[]{:S(2)}, u32[]{:S(2)}) collective-permute-start(bf16[96,2,64]{0,2,1:T(8,128)(2,1)S(1)} %fusion.52), channel_id=1, source_target_pairs={{0,16},{16,0},{32,48},{48,32},{64,80},{80,64},{96,112},{112,96},{1... | collective-permute-start | bytes 73736 | tf_op jit(solution)/shard_map/ppermute | solution.py:17
  409.2 3.1 collective-permute-start.1
  413.1 123.3 %copy-start.10 = (f32[2432]{0:T(1024)S(1)}, f32[2432]{0:T(1024)}, u32[]{:S(2)}) copy-start(f32[2432]{0:T(1024)} %get-tuple-element.48) | copy-start | bytes 29188
  413.1 123.3 %copy-start.11 = (f32[2432]{0:T(1024)S(1)}, f32[2432]{0:T(1024)}, u32[]{:S(2)}) copy-start(f32[2432]{0:T(1024)} %get-tuple-element.49) | copy-start | bytes 29188
  533.7 2.6 copy-start.1
  536.3 2.0 copy-start.12
  536.3 2.0 copy-start.13
  538.2 6.5 copy-start.5
  538.5 5.0 collective-permute-start
  541.3 3.4 collective-permute-start.2
  544.9 3.8 copy-start.6
  544.9 94.5 %copy-start.3 = (bf16[512,152]{0,1:T(8,128)(2,1)S(1)}, bf16[512,152]{0,1:T(8,128)(2,1)}, u32[]{:S(2)}) copy-start(bf16[512,152]{0,1:T(8,128)(2,1)} %param.15) | copy-start | bytes 466948
  548.0 0.7 copy-start.4
  548.0 94.3 %copy-start.15 = (s32[16]{0:T(128)S(1)}, s32[16]{0:T(128)}, u32[]{:S(2)}) copy-start(s32[16]{0:T(128)} %param.18) | copy-start | bytes 196
  548.0 96.2 %copy-start.7 = (bf16[76,64]{0,1:T(8,128)(2,1)S(1)}, bf16[76,64]{0,1:T(8,128)(2,1)}, u32[]{:S(2)}) copy-start(bf16[76,64]{0,1:T(8,128)(2,1)} %param.27) | copy-start | bytes 29188
  548.7 193.6 %all-gather.14.cloned.1.call-start = ((), (), s32[]{:S(2)}) async-start(), calls=%async_computation.3 | async-start | bytes 2646016 | tf_op jit(solution)/shard_map/all_gather | solution.py:140
  642.3 102.6 %copy-start.8 = (f32[2432]{0:T(1024)S(1)}, f32[2432]{0:T(1024)}, u32[]{:S(2)}) copy-start(f32[2432]{0:T(1024)} %get-tuple-element.45) | copy-start | bytes 29188
  642.3 102.6 %copy-start.9 = (f32[2432]{0:T(1024)S(1)}, f32[2432]{0:T(1024)}, u32[]{:S(2)}) copy-start(f32[2432]{0:T(1024)} %get-tuple-element.50) | copy-start | bytes 29188
  642.3 102.6 %copy-start.14 = (f32[512,64]{0,1:T(8,128)S(1)}, f32[512,64]{0,1:T(8,128)}, u32[]{:S(2)}) copy-start(f32[512,64]{0,1:T(8,128)} %param.19) | copy-start | bytes 393220
  742.3 2.6 copy-start.2
Sparse Core Ops, SparseCore 0:
  11.5 266.3 all-reduce.2
  280.2 76.0 all-gather.17
  359.3 68.1 all-gather.15
  430.8 102.8 all-gather.9
  548.8 90.5 all-gather.11
  642.8 99.4 all-gather.13
where the time goes:
time: 754 us
  waiting for transfers between devices  417 us (55%)
  blocking collectives  228 us (30%)
  other arithmetic  51.4 us (7%)
  local copies, waits for them, and re-layouts  16 us (2%)
  between operations  15.9 us (2%)
  starting transfers between devices  13.8 us (2%)
  matrix products  11.6 us (2%)
    psum x1, waiting for transfers between devices, per_device(): mod_all = lax.psum(mod_terms, 'row')  200 us
    all_gather x1, waiting for transfers between devices, per_device(): lax.all_gather(hidden_img, 'col', axis=1, tiled=True)  104 us
    all_gather x1, blocking collectives, per_device(): mod_full = lax.all_gather(mod_own, 'col', axis=1, tiled=True)  77.3 us
    all_gather x1, blocking collectives, per_device(): lax.all_gather(hidden_txt, 'col', axis=1, tiled=True)  61.1 us
    all_gather x1, waiting for transfers between devices, per_device(): residual = lax.all_gather(updated, 'col', axis=1, tiled=True)  51.6 us
    all_gather x1, waiting for transfers between devices, per_device(): full_heads = lax.all_gather(attended, 'col', axis=1, tiled=True)  45.6 us
    all_gather x1, blocking collectives, per_device(): head_full = lax.all_gather(final_weight, 'row', axis=0, tiled=True)  45.2 us
    all_gather x1, blocking collectives, per_device(): lax.all_gather(out_weight, 'row', axis=0, tiled=True)  44.3 us
  transfers between devices with their start and end apart: 10, of which 7 were waited for; matrix products, arithmetic and copies ran while one was open for 8% of the time, Pallas kernels for 0%

commit v1 on v0

--- a/solution.py
+++ b/solution.py
@@ -62,7 +62,8 @@
     mod_terms = jnp.dot(activated, mod_local, preferred_element_type=jnp.float32).reshape(
         activated.shape[0], 7, width_part
     )
-    mod_all = lax.psum(mod_terms, "row")
+    shards = lax.all_gather(mod_terms, "row", axis=0, tiled=False)
+    mod_all = shards.sum(axis=0)
     mod_own = lax.dynamic_index_in_dim(mod_all, request, 0, keepdims=False)
     mod_full = lax.all_gather(mod_own, "col", axis=1, tiled=True)
     img_full, txt_full = (

time: 754 us -> 622 us (0.82)
  waiting for transfers between devices: 417 us -> 232 us
  blocking collectives: 228 us -> 283 us
    psum x1 -> x0, waiting for transfers between devices: 200 us -> none  [per_device(): mod_all = lax.psum(mod_terms, 'row')]
    all_gather x1, waiting for transfers between devices: 104 us -> 0.02 us  [per_device(): lax.all_gather(hidden_img, 'col', axis=1, tiled=True)]
    all_gather x0 -> x1, waiting for transfers between devices: none -> 66.6 us  [per_device(): shards = lax.all_gather(mod_terms, 'row', axis=0, tiled=False)]
    all_gather x1, waiting for transfers between devices: 14.4 us -> 64.1 us  [per_device(): lax.all_gather(qkv_flat, 'row', axis=0, tiled=True)]
    all_gather x1, blocking collectives: 77.3 us -> 117 us  [per_device(): mod_full = lax.all_gather(mod_own, 'col', axis=1, tiled=True)]
    all_gather x1, blocking collectives: 44.3 us -> 58.2 us  [per_device(): lax.all_gather(out_weight, 'row', axis=0, tiled=True)]
    all_gather x1, waiting for transfers between devices: 0.01 us -> 7.82 us  [per_device(): lax.all_gather(kv_flat, 'row', axis=0, tiled=True)]
  transfers between devices with their start and end apart: 10 -> 10, of which waited for: 7 -> 7; matrix products, arithmetic and copies ran while one was open for 8% -> 10% of each run, Pallas kernels for 0% -> 0%
where the time goes in v1:
time: 622 us
  blocking collectives  283 us (45%)
  waiting for transfers between devices  232 us (37%)
  other arithmetic  52.4 us (8%)
  between operations  15.9 us (3%)
  starting transfers between devices  13.3 us (2%)
  local copies, waits for them, and re-layouts  13.2 us (2%)
  matrix products  11.6 us (2%)
    all_gather x1, blocking collectives, per_device(): mod_full = lax.all_gather(mod_own, 'col', axis=1, tiled=True)  117 us
    all_gather x1, waiting for transfers between devices, per_device(): shards = lax.all_gather(mod_terms, 'row', axis=0, tiled=False)  66.6 us
    all_gather x1, waiting for transfers between devices, per_device(): lax.all_gather(qkv_flat, 'row', axis=0, tiled=True)  64.1 us
    all_gather x1, blocking collectives, per_device(): lax.all_gather(hidden_txt, 'col', axis=1, tiled=True)  60.3 us
    all_gather x1, blocking collectives, per_device(): lax.all_gather(out_weight, 'row', axis=0, tiled=True)  58.2 us
    all_gather x1, waiting for transfers between devices, per_device(): residual = lax.all_gather(updated, 'col', axis=1, tiled=True)  49.2 us
    all_gather x1, blocking collectives, per_device(): head_full = lax.all_gather(final_weight, 'row', axis=0, tiled=True)  47.5 us
    add x1, other arithmetic, modulate_full(): return (normed * (1.0 + stretch) + offset).astype(jnp.bfloat16)  42.5 us
  transfers between devices with their start and end apart: 10, of which 7 were waited for; matrix products, arithmetic and copies ran while one was open for 10% of the time, Pallas kernels for 0%

profile of v1, /device:TPU:1, one launch (start us, length us, event | category | flops | bytes accessed | tf_op | source)
XLA Modules:
  0.0 621.8 jit_solution(7362403257920120968)
XLA Ops:
  7.2 0.0 all-gather.22.cloned.1.call-start
  7.2 1.4 reshape.170
  8.7 0.0 all-gather.22.cloned.1.call-update
  8.7 0.0 all-gather.20.cloned.1.call-start
  8.7 0.9 copy.53
  9.6 0.7 reshape.168
  10.3 0.0 all-gather.20.cloned.1.call-update
  10.3 0.0 all-gather.18.cloned.1.call-start
  10.4 1.6 fusion.48
  12.0 0.0 all-gather.18.cloned.1.call-update
  12.0 0.0 all-gather.12.cloned.1.call-start
  12.1 0.5 all-gather.12.cloned.1.call-update
  12.6 0.0 all-gather.14.cloned.1.call-start
  12.7 1.3 dynamic_slice.23
  14.0 0.7 iota_compare_fusion
  14.7 60.3 %all_gather.34 = bf16[96,2432]{0,1:T(8,128)(2,1)S(1)} all-gather(bf16[96,152]{0,1:T(8,128)(2,1)} %param.16), channel_id=1, replica_groups=mesh['row'=32,'col'=16] {'col'}, dimensions={1}, use_global_device_ids=true | all-gather | bytes 496128 | tf_op jit(solution)/shard_map/all_gather | solution.py:71
  75.0 0.3 convert_reduce_fusion.2
  75.3 0.8 slice_bitcast_fusion.3
  76.1 7.8 %all-gather.22.cloned.1.call-done = bf16[32,76,256]{2,1,0:T(8,128)(2,1)} async-done(((bf16[1,76,256]{2,1,0:T(8,128)(2,1)}), bf16[32,76,256]{2,1,0:T(8,128)(2,1)}) %all-gather.22.cloned.1.call-update) | async-done | bytes 1245200 | tf_op jit(solution)/shard_map/all_gather | solution.py:84
  83.9 2.9 reshape.171
  86.9 64.1 %all-gather.20.cloned.1.call-done = bf16[32,76,384]{2,1,0:T(8,128)(2,1)} async-done(((bf16[1,76,384]{2,1,0:T(8,128)(2,1)}), bf16[32,76,384]{2,1,0:T(8,128)(2,1)}) %all-gather.20.cloned.1.call-update) | async-done | bytes 1867792 | tf_op jit(solution)/shard_map/all_gather | solution.py:79
  150.9 2.5 reshape.169
  153.4 66.6 %all-gather.18.cloned.1.call-done = f32[512,7,152]{2,0,1:T(8,128)} async-done(((f32[16,7,152]{2,0,1:T(8,128)}), f32[512,7,152]{2,0,1:T(8,128)}) %all-gather.18.cloned.1.call-update) | async-done | bytes 2179088 | tf_op jit(solution)/shard_map/all_gather | solution.py:65
  220.0 2.5 reduce_sum.99
  222.5 0.1 copy.52
  222.6 116.9 %all-gather.1 = f32[1,7,2432]{1,0,2:T(1,128)S(1)} all-gather(f32[1,7,152]{1,0,2:T(1,128)S(1)} %copy.52), channel_id=3, replica_groups=mesh['row'=32,'col'=16] {'col'}, dimensions={2}, use_global_device_ids=true | all-gather | bytes 72352 | tf_op jit(solution)/shard_map/all_gather | solution.py:68
  339.4 42.5 %fusion.39 = (f32[2432]{0:T(1024)S(1)}, f32[2432]{0:T(1024)S(1)}, f32[2432]{0:T(1024)S(1)}, f32[2432]{0:T(1024)S(1)}, f32[2432]{0:T(1024)S(1)}, /*index=5*/f32[2432]{0:T(1024)S(1)}) fusion(f32[1,7,2432]{1,0,2:T(1,128)S(1)} %all-gather.1), kind=kLoop, calls=%fused_computation.55 | loop fusion | flops 7296 | bytes 116736 | tf_op jit(solution)/shard_map/add | solution.py:24
  382.0 1.3 fusion.42
  383.2 6.6 %collective-permute-start.3 = (bf16[96,2,64]{0,2,1:T(8,128)(2,1)S(1)}, bf16[96,2,64]{0,2,1:T(8,128)(2,1)S(1)}, u32[]{:S(2)}, u32[]{:S(2)}) collective-permute-start(bf16[96,2,64]{0,2,1:T(8,128)(2,1)S(1)} %fusion.52), channel_id=1, source_target_pairs={{0,16},{16,0},{32,48},{48,32},{64,80},{80,64},{96,112},{112,96},{1... | collective-permute-start | bytes 73736 | tf_op jit(solution)/shard_map/ppermute | solution.py:17
  389.9 0.1 multiply_convert_fusion.2
  390.0 2.1 collective-permute-start.1
  392.1 1.0 collective-permute-done.1
  393.1 0.1 broadcast_select_fusion.6
  393.2 0.0 all-gather.12.cloned.1.call-done
  393.2 2.6 convert_reduce_fusion.1
  395.8 1.9 fusion.24
  397.7 0.1 multiply_reduce_fusion
  397.8 2.1 collective-permute-start.2
  399.9 0.1 multiply_convert_fusion
  400.0 2.3 collective-permute-start
  402.3 0.1 concatenate.11
  402.4 0.8 collective-permute-done
  403.3 0.1 concatenate.10
  403.4 3.1 while.10
  403.4 0.6 fusion.66
  404.0 0.4 fusion.67
  404.4 0.6 fusion.68
  405.0 0.5 fusion.66
  405.5 0.4 fusion.67
  405.9 0.6 fusion.68
  406.5 0.6 copy-done.5
  407.2 0.0 all-gather.14.cloned.1.call-update
  407.2 0.0 all-gather.16.cloned.1.call-start
  407.2 58.2 %all_gather.37 = bf16[2048,152]{1,0:T(8,128)(2,1)S(1)} all-gather(bf16[64,152]{1,0:T(8,128)(2,1)S(1)} %copy-done.6), channel_id=1, replica_groups=mesh['row'=32,'col'=16] {'row'}, dimensions={0}, use_global_device_ids=true | all-gather | bytes 642048 | tf_op jit(solution)/shard_map/all_gather | solution.py:136
  465.5 42.4 %all-gather.14.cloned.1.call-done = bf16[512,2048]{0,1:T(8,128)(2,1)} async-done(((bf16[512,128]{0,1:T(8,128)(2,1)}), bf16[512,2048]{0,1:T(8,128)(2,1)}) %all-gather.14.cloned.1.call-update) | async-done | bytes 2097168 | tf_op jit(solution)/shard_map/all_gather | solution.py:133
  507.8 2.8 fusion.41
  510.7 0.0 all-gather.16.cloned.1.call-update
  510.7 0.6 dynamic_slice.24
  512.6 47.5 %all-gather.4 = bf16[32,76,64]{1,2,0:T(8,128)(2,1)S(1)} all-gather(bf16[1,76,64]{1,2,0:T(8,128)(2,1)S(1)} %bitcast.106), channel_id=1, replica_groups=mesh['row'=32,'col'=16] {'row'}, dimensions={0}, use_global_device_ids=true | all-gather | bytes 321024 | tf_op jit(solution)/shard_map/all_gather | solution.py:140
  560.2 0.3 copy.58
  560.5 0.8 reshape.173
  561.4 49.2 %all-gather.16.cloned.1.call-done = bf16[512,2432]{0,1:T(8,128)(2,1)} async-done(((bf16[512,152]{0,1:T(8,128)(2,1)}), bf16[512,2432]{0,1:T(8,128)(2,1)}) %all-gather.16.cloned.1.call-update) | async-done | bytes 2490384 | tf_op jit(solution)/shard_map/all_gather | solution.py:141
  610.6 2.6 convert_reduce_fusion
  613.2 1.8 multiply_add_fusion
  (38 shorter events, 0.3 us)
Async XLA Ops:
  7.2 3.2 copy-start
  7.2 76.8 %all-gather.22.cloned.1.call-start = ((), (), s32[]{:S(2)}) async-start(), calls=%async_computation.5 | async-start | bytes 1351680 | tf_op jit(solution)/shard_map/all_gather | solution.py:84
  8.7 142.2 %all-gather.20.cloned.1.call-start = ((), (), s32[]{:S(2)}) async-start(), calls=%async_computation.4 | async-start | bytes 2027520 | tf_op jit(solution)/shard_map/all_gather | solution.py:79
  10.3 209.7 %all-gather.18.cloned.1.call-start = ((), (), s32[]{:S(2)}) async-start(), calls=%async_computation.3 | async-start | bytes 3784704 | tf_op jit(solution)/shard_map/all_gather | solution.py:65
  12.0 381.2 %all-gather.12.cloned.1.call-start = ((), (), s32[]{:S(2)}) async-start(), calls=%async_computation | async-start | bytes 2646016 | tf_op jit(solution)/shard_map/all_gather | solution.py:70
  12.6 495.2 %all-gather.14.cloned.1.call-start = ((), (), s32[]{:S(2)}) async-start(), calls=%async_computation.1 | async-start | bytes 2228224 | tf_op jit(solution)/shard_map/all_gather | solution.py:133
  339.4 42.5 %copy-start.3 = (bf16[2432,256]{1,0:T(8,128)(2,1)S(1)}, bf16[2432,256]{1,0:T(8,128)(2,1)}, u32[]{:S(2)}) copy-start(bf16[2432,256]{1,0:T(8,128)(2,1)} %reshape.171) | copy-start | bytes 3735556
  383.2 8.9 %collective-permute-start.3 = (bf16[96,2,64]{0,2,1:T(8,128)(2,1)S(1)}, bf16[96,2,64]{0,2,1:T(8,128)(2,1)S(1)}, u32[]{:S(2)}, u32[]{:S(2)}) collective-permute-start(bf16[96,2,64]{0,2,1:T(8,128)(2,1)S(1)} %fusion.52), channel_id=1, source_target_pairs={{0,16},{16,0},{32,48},{48,32},{64,80},{80,64},{96,112},{112,96},{1... | collective-permute-start | bytes 73736 | tf_op jit(solution)/shard_map/ppermute | solution.py:17
  390.0 3.1 collective-permute-start.1
  393.2 2.6 copy-start.1
  395.8 4.1 copy-start.8
  397.8 4.5 collective-permute-start.2
  400.0 3.2 collective-permute-start
  403.4 3.9 copy-start.6
  403.4 104.4 %copy-start.4 = (bf16[512,152]{0,1:T(8,128)(2,1)S(1)}, bf16[512,152]{0,1:T(8,128)(2,1)}, u32[]{:S(2)}) copy-start(bf16[512,152]{0,1:T(8,128)(2,1)} %param.15) | copy-start | bytes 466948
  406.5 0.7 copy-start.5
  406.5 104.2 %copy-start.10 = (s32[16]{0:T(128)S(1)}, s32[16]{0:T(128)}, u32[]{:S(2)}) copy-start(s32[16]{0:T(128)} %param.18) | copy-start | bytes 196
  406.5 106.1 %copy-start.7 = (bf16[76,64]{0,1:T(8,128)(2,1)S(1)}, bf16[76,64]{0,1:T(8,128)(2,1)}, u32[]{:S(2)}) copy-start(bf16[76,64]{0,1:T(8,128)(2,1)} %param.27) | copy-start | bytes 29188
  407.2 203.4 %all-gather.16.cloned.1.call-start = ((), (), s32[]{:S(2)}) async-start(), calls=%async_computation.2 | async-start | bytes 2646016 | tf_op jit(solution)/shard_map/all_gather | solution.py:141
  510.7 102.4 %copy-start.9 = (f32[512,64]{0,1:T(8,128)S(1)}, f32[512,64]{0,1:T(8,128)}, u32[]{:S(2)}) copy-start(f32[512,64]{0,1:T(8,128)} %param.19) | copy-start | bytes 393220
  610.6 2.6 copy-start.2
Sparse Core Ops, SparseCore 0:
  10.2 73.7 all-gather.21
  86.7 64.2 all-gather.19
  153.7 66.2 all-gather.17
  222.9 127.6 all-gather.11
  407.3 100.4 all-gather.13
  510.8 99.7 all-gather.15
